TPU v7x, 512 devices: a whole 4x4x16 slice. The times are simulated.
512 devices in a mesh: leaf: 32 (over z, core), front: 16 (over x, y).
Axes of the slice: x: 4, y: 4, z: 16, core: 2. Of those that a mesh axis runs over, the one named last changes fastest.
Arguments:
- subtree_rhs: bfloat16 [524288, 256], P(('leaf', 'front')), may hold values from -6 to 6
- subtree_inverse: bfloat16 [524288, 1024], P(('leaf', 'front')), as said below
- coupling: bfloat16 [16384, 1024], P(('leaf', 'front')), may hold values from -0.1875 to 0.1875
- rhs_top: bfloat16 [4096, 256], P(('leaf', 'front')), may hold values from -6 to 6
- rhs_mid: bfloat16 [8192, 256], P(('leaf', 'front')), may hold values from -6 to 6
- rhs_low: bfloat16 [16384, 256], P(('leaf', 'front')), may hold values from -6 to 6
- inverse_top: bfloat16 [32, 16, 8, 4096], P(None, 'front', None, 'leaf'), as said below
- inverse_mid: bfloat16 [16, 16, 16, 8192], P(None, 'front', None, 'leaf'), as said below
- inverse_low: bfloat16 [8, 16, 32, 16384], P(None, 'front', None, 'leaf'), as said below
- update_mid: bfloat16 [16, 16, 16, 2, 4096], P(None, 'front', None, None, 'leaf'), may hold values from -0.0625 to 0.0625
- update_low: bfloat16 [8, 16, 32, 2, 8192], P(None, 'front', None, None, 'leaf'), may hold values from -0.0625 to 0.0625
- front_rows: int32 [7], replicated, may hold values from 1024 to 4096, as said below
Outputs:
- solution_sub: bfloat16 [524288, 256], P(('leaf', 'front'))
- solution_top: bfloat16 [4096, 256], P(('leaf', 'front'))
- solution_mid: bfloat16 [8192, 256], P(('leaf', 'front'))
- solution_low: bfloat16 [16384, 256], P(('leaf', 'front'))
Inputs may be any that keep to these rules, and one draw needn't show every extreme that they name: `front_rows`: live rows of the seven fronts in level order; each is a multiple of 128; the root has all 4096 rows, and at least one lowest front has all 4096 rows. `subtree_inverse`: each block of 1024 rows is a lower-triangular matrix with diagonal entries from 0.6 to 1.4. `inverse_top`: each front's block D is lower triangular with diagonal entries from 0.6 to 1.4. `inverse_mid`: each front's block D is lower triangular with diagonal entries from 0.6 to 1.4. `inverse_low`: each front's block D is lower triangular with diagonal entries from 0.6 to 1.4.
All inputs are finite; a program needn't handle non-finite values.
Results may differ from a plain program's by a relative error of at most 0.025.
Values may be sent and summed in bfloat16 or wider, within the bound.
No kernel may reach another device: no remote copies, remote signals or barrier semaphores. Data moves between devices by JAX's collectives and lax.ppermute only.
A program may use at most 64 MiB of HBM per device.

v0:
```python
import jax
import jax.numpy as jnp
from jax import lax
from jax.sharding import PartitionSpec as P


def partner(array, axis, distance):
    return lax.ppermute(array, axis, [(i, i ^ 1 << distance) for i in range(lax.axis_size(axis))])


def live_mask(front_rows, heap_start, groups, pieces):
    leaf_pos = lax.axis_index("leaf")
    front_pos = lax.axis_index("front")
    member = leaf_pos % groups
    node_pos = leaf_pos // groups
    lookup = jnp.arange(front_rows.shape[0], dtype=jnp.int32)
    live_rows = jnp.sum(jnp.where(lookup == heap_start + node_pos, front_rows, 0))
    front_ways = lax.axis_size("front")
    row_offset = (member * front_ways + front_pos) * pieces
    row_ids = row_offset + jnp.arange(pieces, dtype=jnp.int32)
    return (row_ids < live_rows)[:, None]


def group_gather(block, groups):
    leaf_pos = lax.axis_index("leaf")
    gathered = lax.all_gather(block, "leaf", axis=0, tiled=True)
    start_row = leaf_pos // groups * groups * block.shape[0]
    return lax.dynamic_slice_in_dim(gathered, start_row, groups * block.shape[0], 0)


def group_reduce(partial_value, groups):
    leaf_pos = lax.axis_index("leaf")
    current = partial_value.reshape(groups, -1, partial_value.shape[-1])
    for bit_pos in reversed(range(groups.bit_length() - 1)):
        half_count = current.shape[0] // 2
        lower_half = current[:half_count]
        upper_half = current[half_count:]
        upper_bit = leaf_pos // (1 << bit_pos) % 2
        kept_half = jnp.where(upper_bit == 0, lower_half, upper_half)
        sent_half = jnp.where(upper_bit == 0, upper_half, lower_half)
        current = kept_half + partner(sent_half.astype(jnp.bfloat16), "leaf", bit_pos).astype(
            sent_half.dtype
        )
    return current[0]


def forward_front(right_block, inverse, row_mask):
    groups = inverse.shape[0]
    pieces = inverse.shape[2]
    local_inverse = inverse.reshape(groups * pieces, inverse.shape[3])
    columns = group_gather(right_block, groups)
    summed = lax.psum_scatter(
        lax.dot_general(
            local_inverse, columns, (((0,), (0,)), ((), ())), preferred_element_type=jnp.float32
        ).astype(jnp.bfloat16),
        "front",
        scatter_dimension=0,
        tiled=True,
    ).astype(jnp.float32)
    return jnp.where(row_mask, summed, 0.0).astype(jnp.bfloat16)


def forward_update(child_solved, update, parent_rhs, parent_mask):
    groups = update.shape[0]
    pieces = update.shape[2]
    half_rows = update.shape[4]
    local_update = update.reshape(groups * pieces, 2 * half_rows)
    columns = group_gather(child_solved, groups)
    products = lax.dot_general(
        local_update, columns, (((0,), (0,)), ((), ())), preferred_element_type=jnp.float32
    )
    products = products.reshape(2, half_rows, columns.shape[1])
    parity = lax.axis_index("leaf") // groups % 2
    bit_pos = groups.bit_length() - 1
    kept_half = lax.dynamic_index_in_dim(products, parity, 0, keepdims=False)
    sent_half = lax.dynamic_index_in_dim(products, 1 - parity, 0, keepdims=False)
    both_sums = kept_half + partner(sent_half.astype(jnp.bfloat16), "leaf", bit_pos).astype(
        sent_half.dtype
    )
    summed = lax.psum_scatter(
        both_sums.astype(jnp.bfloat16), "front", scatter_dimension=0, tiled=True
    ).astype(jnp.float32)
    return jnp.where(parent_mask, parent_rhs.astype(jnp.float32) - summed, 0.0).astype(jnp.bfloat16)


def backward_front(solved_block, inverse, row_mask):
    groups = inverse.shape[0]
    pieces = inverse.shape[2]
    local_inverse = inverse.reshape(groups * pieces, inverse.shape[3])

    def add_rows(running, piece_rows, start_row):
        return jnp.dot(local_inverse, piece_rows, preferred_element_type=jnp.float32)

    initial = jnp.zeros((groups * pieces, solved_block.shape[1]), jnp.float32)
    partial_value = add_rows(
        initial, lax.all_gather(solved_block, "front", axis=0, tiled=True), jnp.int32(0)
    )
    summed = group_reduce(partial_value, groups)
    return jnp.where(row_mask, summed, 0.0).astype(jnp.bfloat16)


def backward_update(child_forward, update, parent_solution, row_mask):
    groups = update.shape[0]
    pieces = update.shape[2]
    half_rows = update.shape[4]
    local_update = update.reshape(groups * pieces, 2, half_rows)
    parity = lax.axis_index("leaf") // groups % 2
    bit_pos = groups.bit_length() - 1
    sibling_block = partner(parent_solution, "leaf", bit_pos)
    own_update = lax.dynamic_index_in_dim(local_update, parity, 1, keepdims=False)
    other_update = lax.dynamic_index_in_dim(local_update, 1 - parity, 1, keepdims=False)

    def add_rows(running, pieces_pair, start_row):
        own_rows, other_rows = pieces_pair
        running = jnp.dot(own_update, own_rows, preferred_element_type=jnp.float32)
        return running + jnp.dot(other_update, other_rows, preferred_element_type=jnp.float32)

    initial = jnp.zeros((groups * pieces, parent_solution.shape[1]), jnp.float32)
    partial_value = add_rows(
        initial,
        (
            lax.all_gather(parent_solution, "front", axis=0, tiled=True),
            lax.all_gather(sibling_block, "front", axis=0, tiled=True),
        ),
        jnp.int32(0),
    )
    summed = group_reduce(partial_value, groups)
    return jnp.where(row_mask, child_forward.astype(jnp.float32) - summed, 0.0).astype(jnp.bfloat16)


def shards(
    subtree_rhs,
    subtree_inverse,
    coupling,
    rhs_top,
    rhs_mid,
    rhs_low,
    inverse_top,
    inverse_mid,
    inverse_low,
    update_mid,
    update_low,
    front_rows,
):
    below_solved = jnp.dot(subtree_inverse, subtree_rhs, preferred_element_type=jnp.float32).astype(
        jnp.bfloat16
    )
    mask_top = live_mask(front_rows, 0, inverse_top.shape[0], rhs_top.shape[0])
    mask_mid = live_mask(front_rows, 1, inverse_mid.shape[0], rhs_mid.shape[0])
    mask_low = live_mask(front_rows, 3, inverse_low.shape[0], rhs_low.shape[0])
    pushed = jnp.dot(coupling, below_solved, preferred_element_type=jnp.float32)
    right_low = jnp.where(mask_low, rhs_low.astype(jnp.float32) - pushed, 0.0).astype(jnp.bfloat16)
    forward_low = forward_front(right_low, inverse_low, mask_low)
    right_mid = forward_update(forward_low, update_low, rhs_mid, mask_mid)
    forward_mid = forward_front(right_mid, inverse_mid, mask_mid)
    right_top = forward_update(forward_mid, update_mid, rhs_top, mask_top)
    forward_top = forward_front(right_top, inverse_top, mask_top)
    solution_top = backward_front(forward_top, inverse_top, mask_top)
    residual_mid = backward_update(forward_mid, update_mid, solution_top, mask_mid)
    solution_mid = backward_front(residual_mid, inverse_mid, mask_mid)
    residual_low = backward_update(forward_low, update_low, solution_mid, mask_low)
    solution_low = backward_front(residual_low, inverse_low, mask_low)
    moved = lax.dot_general(
        coupling, solution_low, (((0,), (0,)), ((), ())), preferred_element_type=jnp.float32
    )
    shifted = (below_solved.astype(jnp.float32) - moved).astype(jnp.bfloat16)
    solution_sub = lax.dot_general(
        subtree_inverse, shifted, (((0,), (0,)), ((), ())), preferred_element_type=jnp.float32
    ).astype(jnp.bfloat16)
    return (solution_sub, solution_top, solution_mid, solution_low)


def solution(mesh):
    placed = (
        P(("leaf", "front"), None),
        P(("leaf", "front"), None),
        P(("leaf", "front"), None),
        P(("leaf", "front"), None),
        P(("leaf", "front"), None),
        P(("leaf", "front"), None),
        P(None, "front", None, "leaf"),
        P(None, "front", None, "leaf"),
        P(None, "front", None, "leaf"),
        P(None, "front", None, None, "leaf"),
        P(None, "front", None, None, "leaf"),
        P(),
    )
    return jax.shard_map(
        shards,
        mesh=mesh,
        in_specs=placed,
        out_specs=(
            P(("leaf", "front"), None),
            P(("leaf", "front"), None),
            P(("leaf", "front"), None),
            P(("leaf", "front"), None),
        ),
        check_vma=False,
    )
```

profile of v0, /device:TPU:1, one launch (start us, length us, event | category | flops | bytes accessed | tf_op | source)
XLA Modules:
  0.0 1013.0 jit_solution(10693021480637807636)
XLA Ops:
  12.2 39.0 %all_gather.36 = bf16[1024,256]{1,0:T(8,128)(2,1)S(1)} all-gather(bf16[32,256]{1,0:T(8,128)(2,1)S(1)} %fusion.8), channel_id=1, replica_groups=mesh['leaf'=32,'front'=16] {'leaf'}, dimensions={0}, use_global_device_ids=true | all-gather | bytes 540672 | tf_op jit(solution)/shard_map/all_gather | solution.py:26
  52.4 81.3 %reduce-scatter.10.cloned.1.call-done = bf16[32,256]{1,0:T(8,128)(2,1)} async-done(((bf16[512,256]{1,0:T(8,128)(2,1)}), bf16[32,256]{1,0:T(8,128)(2,1)}) %reduce-scatter.10.cloned.1.call-update) | async-done | bytes 16400 | tf_op jit(solution)/shard_map/reduce_scatter | solution.py:52
  134.5 34.5 %all_gather.37 = bf16[1024,256]{1,0:T(8,128)(2,1)S(1)} all-gather(bf16[32,256]{1,0:T(8,128)(2,1)S(1)} %select_convert_fusion.15), channel_id=1, replica_groups=mesh['leaf'=32,'front'=16] {'leaf'}, dimensions={0}, use_global_device_ids=true | all-gather | bytes 540672 | tf_op jit(solution)/shard_map/all_gather | solution.py:26
  169.9 4.7 collective-permute-start
  174.9 14.5 %collective-permute-done = bf16[256,256]{0,1:T(8,128)(2,1)} collective-permute-done((bf16[256,256]{0,1:T(8,128)(2,1)S(1)}, bf16[256,256]{0,1:T(8,128)(2,1)}, u32[]{:S(2)}, u32[]{:S(2)}) %collective-permute-start) | collective-permute-done | bytes 131104 | tf_op jit(solution)/shard_map/ppermute | solution.py:8
  191.8 80.4 %reduce-scatter.12.cloned.1.call-done = bf16[16,256]{1,0:T(8,128)(2,1)} async-done(((bf16[256,256]{1,0:T(8,128)(2,1)}), bf16[16,256]{1,0:T(8,128)(2,1)}) %reduce-scatter.12.cloned.1.call-update) | async-done | bytes 8208 | tf_op jit(solution)/shard_map/reduce_scatter | solution.py:80
  273.0 34.1 %all_gather.38 = bf16[512,256]{1,0:T(8,128)(2,1)S(1)} all-gather(bf16[16,256]{1,0:T(8,128)(2,1)S(1)} %select_convert_fusion.20), channel_id=1, replica_groups=mesh['leaf'=32,'front'=16] {'leaf'}, dimensions={0}, use_global_device_ids=true | all-gather | bytes 270336 | tf_op jit(solution)/shard_map/all_gather | solution.py:26
  308.2 80.8 %reduce-scatter.14.cloned.1.call-done = bf16[16,256]{1,0:T(8,128)(2,1)} async-done(((bf16[256,256]{1,0:T(8,128)(2,1)}), bf16[16,256]{1,0:T(8,128)(2,1)}) %reduce-scatter.14.cloned.1.call-update) | async-done | bytes 8208 | tf_op jit(solution)/shard_map/reduce_scatter | solution.py:52
  389.8 34.1 %all_gather.39 = bf16[512,256]{1,0:T(8,128)(2,1)S(1)} all-gather(bf16[16,256]{1,0:T(8,128)(2,1)S(1)} %select_convert_fusion.19), channel_id=1, replica_groups=mesh['leaf'=32,'front'=16] {'leaf'}, dimensions={0}, use_global_device_ids=true | all-gather | bytes 270336 | tf_op jit(solution)/shard_map/all_gather | solution.py:26
  424.1 8.9 collective-permute-start.1
  439.6 108.8 %all-reduce.5.cloned.1.call-done = bf16[128,256]{1,0:T(8,128)(2,1)} async-done(((bf16[128,256]{1,0:T(8,128)(2,1)}), bf16[128,256]{1,0:T(8,128)(2,1)}) %all-reduce.5.cloned.1.call-update) | async-done | bytes 65552
  549.2 33.4 %all_gather.40 = bf16[256,256]{1,0:T(8,128)(2,1)S(1)} all-gather(bf16[8,256]{1,0:T(8,128)(2,1)S(1)} %select_convert_fusion.23), channel_id=1, replica_groups=mesh['leaf'=32,'front'=16] {'leaf'}, dimensions={0}, use_global_device_ids=true | all-gather | bytes 135168 | tf_op jit(solution)/shard_map/all_gather | solution.py:26
  584.5 105.7 %all-reduce.7.cloned.1.call-done = bf16[128,256]{1,0:T(8,128)(2,1)} async-done(((bf16[128,256]{1,0:T(8,128)(2,1)}), bf16[128,256]{1,0:T(8,128)(2,1)}) %all-reduce.7.cloned.1.call-update) | async-done | bytes 65552
  690.9 17.5 %all_gather.41 = bf16[128,256]{1,0:T(8,128)(2,1)S(1)} all-gather(bf16[8,256]{1,0:T(8,128)(2,1)S(1)} %select_convert_fusion.22), channel_id=1, replica_groups=mesh['leaf'=32,'front'=16] {'front'}, dimensions={0}, use_global_device_ids=true | all-gather | bytes 69632 | tf_op jit(solution)/shard_map/all_gather | solution.py:96
  709.4 12.5 %collective-permute-start.2 = (bf16[16,8,256]{2,1,0:T(8,128)(2,1)S(1)}, bf16[16,8,256]{2,1,0:T(8,128)(2,1)S(1)}, u32[]{:S(2)}, u32[]{:S(2)}) collective-permute-start(bf16[16,8,256]{2,1,0:T(8,128)(2,1)S(1)} %fusion.26), channel_id=1, source_target_pairs={{0,256},{16,272},{32,288},{48,304},{64,320},{80,336},{96,352},{112... | collective-permute-start | bytes 196616 | tf_op jit(solution)/shard_map/ppermute | solution.py:8
  723.9 7.9 collective-permute-start.3
  745.7 12.3 %collective-permute-start.6 = (bf16[1,8,256]{2,1,0:T(8,128)(2,1)S(1)}, bf16[1,8,256]{2,1,0:T(8,128)(2,1)S(1)}, u32[]{:S(2)}, u32[]{:S(2)}) collective-permute-start(bf16[1,8,256]{2,1,0:T(8,128)(2,1)S(1)} %select_convert_fusion.21), channel_id=1, source_target_pairs={{0,16},{16,0},{32,48},{48,32},{64,80},{80,64},{96,112},{112,96},{1... | collective-permute-start | bytes 12296 | tf_op jit(solution)/shard_map/ppermute | solution.py:8
  758.8 15.9 %all_gather.42 = bf16[128,256]{1,0:T(8,128)(2,1)S(1)} all-gather(bf16[8,256]{1,0:T(8,128)(2,1)S(1)} %fusion.40), channel_id=1, replica_groups=mesh['leaf'=32,'front'=16] {'front'}, dimensions={0}, use_global_device_ids=true | all-gather | bytes 69632 | tf_op jit(solution)/shard_map/all_gather | solution.py:122
  774.7 13.4 %collective-permute-start.7 = (bf16[8,256]{1,0:T(8,128)(2,1)S(1)}, bf16[8,256]{1,0:T(8,128)(2,1)S(1)}, u32[]{:S(2)}, u32[]{:S(2)}) collective-permute-start(bf16[8,256]{1,0:T(8,128)(2,1)S(1)} %fusion.40), channel_id=1, source_target_pairs={{0,256},{16,272},{32,288},{48,304},{64,320},{80,336},{96,352},{112... | collective-permute-start | bytes 12296 | tf_op jit(solution)/shard_map/ppermute | solution.py:8
  789.1 17.8 %all_gather.43 = bf16[128,256]{1,0:T(8,128)(2,1)S(1)} all-gather(bf16[8,256]{1,0:T(8,128)(2,1)S(1)} %collective-permute-done.7), channel_id=1, replica_groups=mesh['leaf'=32,'front'=16] {'front'}, dimensions={0}, use_global_device_ids=true | all-gather | bytes 69632 | tf_op jit(solution)/shard_map/all_gather | solution.py:123
  807.1 5.3 collective-permute-start.8
  812.5 5.2 collective-permute-done.8
  828.0 16.8 %collective-permute-start.11 = (bf16[1,16,256]{2,1,0:T(8,128)(2,1)S(1)}, bf16[1,16,256]{2,1,0:T(8,128)(2,1)S(1)}, u32[]{:S(2)}, u32[]{:S(2)}) collective-permute-start(bf16[1,16,256]{2,1,0:T(8,128)(2,1)S(1)} %select_convert_fusion.17), channel_id=1, source_target_pairs={{0,16},{16,0},{32,48},{48,32},{64,80},{80,64},{96,112},{112,96},{1... | collective-permute-start | bytes 24584 | tf_op jit(solution)/shard_map/ppermute | solution.py:8
  845.7 16.0 %all_gather.44 = bf16[256,256]{1,0:T(8,128)(2,1)S(1)} all-gather(bf16[16,256]{1,0:T(8,128)(2,1)S(1)} %fusion.39), channel_id=1, replica_groups=mesh['leaf'=32,'front'=16] {'front'}, dimensions={0}, use_global_device_ids=true | all-gather | bytes 139264 | tf_op jit(solution)/shard_map/all_gather | solution.py:96
  866.4 5.5 collective-permute-done.12
  873.9 5.0 collective-permute-done.13
  883.4 10.0 collective-permute-start.15
  894.3 17.4 %all_gather.45 = bf16[256,256]{1,0:T(8,128)(2,1)S(1)} all-gather(bf16[16,256]{1,0:T(8,128)(2,1)S(1)} %fusion.37), channel_id=1, replica_groups=mesh['leaf'=32,'front'=16] {'front'}, dimensions={0}, use_global_device_ids=true | all-gather | bytes 139264 | tf_op jit(solution)/shard_map/all_gather | solution.py:122
  920.0 16.0 %all_gather.46 = bf16[256,256]{1,0:T(8,128)(2,1)S(1)} all-gather(bf16[16,256]{1,0:T(8,128)(2,1)S(1)} %collective-permute-done.16), channel_id=1, replica_groups=mesh['leaf'=32,'front'=16] {'front'}, dimensions={0}, use_global_device_ids=true | all-gather | bytes 139264 | tf_op jit(solution)/shard_map/all_gather | solution.py:123
  947.5 16.4 %collective-permute-start.19 = (bf16[1,32,256]{2,1,0:T(8,128)(2,1)S(1)}, bf16[1,32,256]{2,1,0:T(8,128)(2,1)S(1)}, u32[]{:S(2)}, u32[]{:S(2)}) collective-permute-start(bf16[1,32,256]{2,1,0:T(8,128)(2,1)S(1)} %select_convert_fusion.11), channel_id=1, source_target_pairs={{0,16},{16,0},{32,48},{48,32},{64,80},{80,64},{96,112},{112,96},{1... | collective-permute-start | bytes 49160 | tf_op jit(solution)/shard_map/ppermute | solution.py:8
  964.8 17.5 %all_gather.47 = bf16[512,256]{1,0:T(8,128)(2,1)S(1)} all-gather(bf16[32,256]{1,0:T(8,128)(2,1)S(1)} %fusion.36), channel_id=1, replica_groups=mesh['leaf'=32,'front'=16] {'front'}, dimensions={0}, use_global_device_ids=true | all-gather | bytes 278528 | tf_op jit(solution)/shard_map/all_gather | solution.py:96
  993.4 10.1 collective-permute-start.22
  (161 shorter events, 98.9 us)
Async XLA Ops:
  7.2 126.5 %reduce-scatter.10.cloned.1.call-start = ((), (), s32[]{:S(2)}) async-start(), calls=%async_computation.3 | async-start | bytes 278528 | tf_op jit(solution)/shard_map/reduce_scatter | solution.py:52
  52.3 219.9 %reduce-scatter.12.cloned.1.call-start = ((), (), s32[]{:S(2)}) async-start(), calls=%async_computation.4 | async-start | bytes 139264 | tf_op jit(solution)/shard_map/reduce_scatter | solution.py:80
  169.3 137.9 %copy-start.7 = (bf16[16,1,16,256]{3,2,1,0:T(8,128)(2,1)S(1)}, bf16[16,1,16,256]{3,2,1,0:T(8,128)(2,1)}, u32[]{:S(2)}) copy-start(bf16[16,1,16,256]{3,2,1,0:T(8,128)(2,1)} %param.19) | copy-start | bytes 393220
  169.6 254.2 %copy-start.4 = (bf16[16,1,16,2,128]{4,3,2,1,0:T(2,128)(2,1)S(1)}, bf16[16,1,16,2,128]{4,3,2,1,0:T(2,128)(2,1)}, u32[]{:S(2)}) copy-start(bf16[16,1,16,2,128]{4,3,2,1,0:T(2,128)(2,1)} %param.21) | copy-start | bytes 393220
  169.9 378.6 %copy-start.17 = (bf16[8,256]{1,0:T(8,128)(2,1)S(1)}, bf16[8,256]{1,0:T(8,128)(2,1)}, u32[]{:S(2)}) copy-start(bf16[8,256]{1,0:T(8,128)(2,1)} %param.15) | copy-start | bytes 12292
  169.9 19.4 %collective-permute-start = (bf16[256,256]{0,1:T(8,128)(2,1)S(1)}, bf16[256,256]{0,1:T(8,128)(2,1)}, u32[]{:S(2)}, u32[]{:S(2)}) collective-permute-start(bf16[256,256]{0,1:T(8,128)(2,1)S(1)} %bitcast.156), channel_id=1, source_target_pairs={{0,128},{16,144},{32,160},{48,176},{64,192},{80,208},{96,224},{112... | collective-permute-start | bytes 393224 | tf_op jit(solution)/shard_map/ppermute | solution.py:8
  191.1 197.9 %reduce-scatter.14.cloned.1.call-start = ((), (), s32[]{:S(2)}) async-start(), calls=%async_computation.5 | async-start | bytes 139264 | tf_op jit(solution)/shard_map/reduce_scatter | solution.py:52
  308.2 240.3 %all-reduce.5.cloned.1.call-start = ((), (), s32[]{:S(2)}) async-start(), calls=%async_computation.6 | async-start | bytes 131072
  424.1 14.1 %collective-permute-start.1 = (bf16[128,256]{1,0:T(8,128)(2,1)S(1)}, bf16[128,256]{1,0:T(8,128)(2,1)S(1)}, u32[]{:S(2)}, u32[]{:S(2)}) collective-permute-start(bf16[128,256]{1,0:T(8,128)(2,1)S(1)} %fusion.25), channel_id=1, source_target_pairs={{0,256},{16,272},{32,288},{48,304},{64,320},{80,336},{96,352},{112... | collective-permute-start | bytes 196616 | tf_op jit(solution)/shard_map/ppermute | solution.py:8
  438.9 251.2 %all-reduce.7.cloned.1.call-start = ((), (), s32[]{:S(2)}) async-start(), calls=%async_computation.7 | async-start | bytes 131072
  709.4 136.3 %copy-start.12 = (bf16[16,256]{1,0:T(8,128)(2,1)S(1)}, bf16[16,256]{1,0:T(8,128)(2,1)}, u32[]{:S(2)}) copy-start(bf16[16,256]{1,0:T(8,128)(2,1)} %reduce-scatter.14.cloned.1.call-done) | copy-start | bytes 24580
  709.4 14.5 %collective-permute-start.2 = (bf16[16,8,256]{2,1,0:T(8,128)(2,1)S(1)}, bf16[16,8,256]{2,1,0:T(8,128)(2,1)S(1)}, u32[]{:S(2)}, u32[]{:S(2)}) collective-permute-start(bf16[16,8,256]{2,1,0:T(8,128)(2,1)S(1)} %fusion.26), channel_id=1, source_target_pairs={{0,256},{16,272},{32,288},{48,304},{64,320},{80,336},{96,352},{112... | collective-permute-start | bytes 196616 | tf_op jit(solution)/shard_map/ppermute | solution.py:8
  723.9 11.9 %collective-permute-start.3 = (bf16[8,8,256]{2,1,0:T(8,128)(2,1)S(1)}, bf16[8,8,256]{2,1,0:T(8,128)(2,1)S(1)}, u32[]{:S(2)}, u32[]{:S(2)}) collective-permute-start(bf16[8,8,256]{2,1,0:T(8,128)(2,1)S(1)} %select_convert_fusion.9), channel_id=1, source_target_pairs={{0,128},{16,144},{32,160},{48,176},{64,192},{80,208},{96,224},{112... | collective-permute-start | bytes 98312 | tf_op jit(solution)/shard_map/ppermute | solution.py:8
  735.8 5.4 collective-permute-start.4
  741.2 4.4 collective-permute-start.5
  745.7 13.1 %collective-permute-start.6 = (bf16[1,8,256]{2,1,0:T(8,128)(2,1)S(1)}, bf16[1,8,256]{2,1,0:T(8,128)(2,1)S(1)}, u32[]{:S(2)}, u32[]{:S(2)}) collective-permute-start(bf16[1,8,256]{2,1,0:T(8,128)(2,1)S(1)} %select_convert_fusion.21), channel_id=1, source_target_pairs={{0,16},{16,0},{32,48},{48,32},{64,80},{80,64},{96,112},{112,96},{1... | collective-permute-start | bytes 12296 | tf_op jit(solution)/shard_map/ppermute | solution.py:8
  774.7 14.4 %collective-permute-start.7 = (bf16[8,256]{1,0:T(8,128)(2,1)S(1)}, bf16[8,256]{1,0:T(8,128)(2,1)S(1)}, u32[]{:S(2)}, u32[]{:S(2)}) collective-permute-start(bf16[8,256]{1,0:T(8,128)(2,1)S(1)} %fusion.40), channel_id=1, source_target_pairs={{0,256},{16,272},{32,288},{48,304},{64,320},{80,336},{96,352},{112... | collective-permute-start | bytes 12296 | tf_op jit(solution)/shard_map/ppermute | solution.py:8
  807.1 10.5 %collective-permute-start.8 = (bf16[8,16,256]{2,1,0:T(8,128)(2,1)S(1)}, bf16[8,16,256]{2,1,0:T(8,128)(2,1)S(1)}, u32[]{:S(2)}, u32[]{:S(2)}) collective-permute-start(bf16[8,16,256]{2,1,0:T(8,128)(2,1)S(1)} %bitcast.159), channel_id=1, source_target_pairs={{0,128},{16,144},{32,160},{48,176},{64,192},{80,208},{96,224},{112... | collective-permute-start | bytes 196616 | tf_op jit(solution)/shard_map/ppermute | solution.py:8
  817.6 5.6 collective-permute-start.9
  823.2 4.8 collective-permute-start.10
  828.0 17.6 %collective-permute-start.11 = (bf16[1,16,256]{2,1,0:T(8,128)(2,1)S(1)}, bf16[1,16,256]{2,1,0:T(8,128)(2,1)S(1)}, u32[]{:S(2)}, u32[]{:S(2)}) collective-permute-start(bf16[1,16,256]{2,1,0:T(8,128)(2,1)S(1)} %select_convert_fusion.17), channel_id=1, source_target_pairs={{0,16},{16,0},{32,48},{48,32},{64,80},{80,64},{96,112},{112,96},{1... | collective-permute-start | bytes 24584 | tf_op jit(solution)/shard_map/ppermute | solution.py:8
  862.0 10.0 collective-permute-start.12
  872.0 6.9 collective-permute-start.13
  878.9 4.5 collective-permute-start.14
  883.4 10.8 %collective-permute-start.15 = (bf16[1,16,256]{2,1,0:T(8,128)(2,1)S(1)}, bf16[1,16,256]{2,1,0:T(8,128)(2,1)S(1)}, u32[]{:S(2)}, u32[]{:S(2)}) collective-permute-start(bf16[1,16,256]{2,1,0:T(8,128)(2,1)S(1)} %select_convert_fusion.16), channel_id=1, source_target_pairs={{0,16},{16,0},{32,48},{48,32},{64,80},{80,64},{96,112},{112,96},{1... | collective-permute-start | bytes 24584 | tf_op jit(solution)/shard_map/ppermute | solution.py:8
  911.7 8.3 collective-permute-start.16
  936.2 6.3 collective-permute-start.17
  942.5 5.0 collective-permute-start.18
  947.5 17.2 %collective-permute-start.19 = (bf16[1,32,256]{2,1,0:T(8,128)(2,1)S(1)}, bf16[1,32,256]{2,1,0:T(8,128)(2,1)S(1)}, u32[]{:S(2)}, u32[]{:S(2)}) collective-permute-start(bf16[1,32,256]{2,1,0:T(8,128)(2,1)S(1)} %select_convert_fusion.11), channel_id=1, source_target_pairs={{0,16},{16,0},{32,48},{48,32},{64,80},{80,64},{96,112},{112,96},{1... | collective-permute-start | bytes 49160 | tf_op jit(solution)/shard_map/ppermute | solution.py:8
  982.6 6.1 collective-permute-start.20
  988.7 4.7 collective-permute-start.21
  993.4 10.9 %collective-permute-start.22 = (bf16[1,32,256]{2,1,0:T(8,128)(2,1)S(1)}, bf16[1,32,256]{2,1,0:T(8,128)(2,1)S(1)}, u32[]{:S(2)}, u32[]{:S(2)}) collective-permute-start(bf16[1,32,256]{2,1,0:T(8,128)(2,1)S(1)} %select_convert_fusion.10), channel_id=1, source_target_pairs={{0,16},{16,0},{32,48},{48,32},{64,80},{80,64},{96,112},{112,96},{1... | collective-permute-start | bytes 49160 | tf_op jit(solution)/shard_map/ppermute | solution.py:8
  (15 other events, 717.9 us)
Sparse Core Ops, SparseCore 0:
  52.4 81.2 reduce-scatter.9
  191.2 81.0 reduce-scatter.11
  308.3 80.6 reduce-scatter.13
  439.0 109.3 all-reduce.4
  584.6 105.5 all-reduce.6
where the time goes:
time: 1010 us
  waiting for transfers between devices  534 us (53%)
  blocking collectives  293 us (29%)
  starting transfers between devices  147 us (15%)
  between operations  15.4 us (2%)
    unnamed x7, waiting for transfers between devices  215 us
    all_gather x5, blocking collectives, group_gather(): gathered = lax.all_gather(block, 'leaf', axis=0, tiled=True)  175 us
    reduce_scatter x2, waiting for transfers between devices, forward_front(): lax.psum_scatter(lax.dot_general(local_inverse, columns, (((0,), (0,)), (...  162 us
    ppermute x23, starting transfers between devices, partner(): lax.ppermute(array, axis, [(i, i ^ 1 << distance) for i in range(lax.axis...  146 us
    reduce_scatter x1, waiting for transfers between devices, forward_update(): lax.psum_scatter(both_sums.astype(jnp.bfloat16), 'front', scatter_dimensi...  80.4 us
    ppermute x23, waiting for transfers between devices, partner(): lax.ppermute(array, axis, [(i, i ^ 1 << distance) for i in range(lax.axis...  76.8 us
    all_gather x3, blocking collectives, backward_front(): lax.all_gather(solved_block, 'front', axis=0, tiled=True)  51 us
    all_gather x2, blocking collectives, backward_update(): lax.all_gather(sibling_block, 'front', axis=0, tiled=True)  33.8 us
  transfers between devices with their start and end apart: 28, of which 28 were waited for; matrix products, arithmetic and copies ran while one was open for 0% of the time, Pallas kernels for 0%

commit v1 on v0

--- a/solution.py
+++ b/solution.py
@@ -2,6 +2,22 @@
 import jax.numpy as jnp
 from jax import lax
 from jax.sharding import PartitionSpec as P
+
+
+def ring_gather(x, axis, dim):
+    ways, here, step = (lax.axis_size(axis), lax.axis_index(axis), x.shape[dim])
+    lengths = [n * ways if d == dim else n for d, n in enumerate(x.shape)]
+    full = lax.dynamic_update_slice_in_dim(jnp.zeros(lengths, x.dtype), x, here * step, axis=dim)
+    going_up = going_down = x
+    for far in range(1, ways // 2 + 1):
+        going_up = lax.ppermute(going_up, axis, [(d, (d + 1) % ways) for d in range(ways)])
+        full = lax.dynamic_update_slice_in_dim(full, going_up, (here - far) % ways * step, axis=dim)
+        if 2 * far < ways:
+            going_down = lax.ppermute(going_down, axis, [(d, (d - 1) % ways) for d in range(ways)])
+            full = lax.dynamic_update_slice_in_dim(
+                full, going_down, (here + far) % ways * step, axis=dim
+            )
+    return full
 
 
 def partner(array, axis, distance):
@@ -120,7 +136,7 @@
         initial,
         (
             lax.all_gather(parent_solution, "front", axis=0, tiled=True),
-            lax.all_gather(sibling_block, "front", axis=0, tiled=True),
+            ring_gather(sibling_block, "front", 0),
         ),
         jnp.int32(0),
     )

time: 1010 us -> 1120 us (1.11)
  starting transfers between devices: 147 us -> 271 us
  blocking collectives: 293 us -> 258 us
    ppermute x0 -> x30, starting transfers between devices: none -> 124 us  [the longest x14 92.7 us: ring_gather(): lax.ppermute(going_down, axis, [(d, (d - 1) % ways) for d in range(ways)])]
    all_gather x2 -> x0, blocking collectives: 33.8 us -> none  [backward_update(): lax.all_gather(sibling_block, 'front', axis=0, tiled=True)]
    ppermute x0 -> x30, waiting for transfers between devices: none -> 11.5 us  [the longest x16 11.5 us: ring_gather(): lax.ppermute(going_up, axis, [(d, (d + 1) % ways) for d in range(ways)])]
  transfers between devices with their start and end apart: 28 -> 58, of which waited for: 28 -> 30; matrix products, arithmetic and copies ran while one was open for 0% -> 0% of each run, Pallas kernels for 0% -> 0%
where the time goes in v1:
time: 1120 us; the launch traced here: 1110 us
  waiting for transfers between devices  544 us (49%)
  starting transfers between devices  271 us (24%)
  blocking collectives  258 us (23%)
  between operations  16.6 us (1%)
    unnamed x7, waiting for transfers between devices  215 us
    all_gather x5, blocking collectives, group_gather(): gathered = lax.all_gather(block, 'leaf', axis=0, tiled=True)  175 us
    reduce_scatter x2, waiting for transfers between devices, forward_front(): lax.psum_scatter(lax.dot_general(local_inverse, columns, (((0,), (0,)), (...  162 us
    ppermute x23, starting transfers between devices, partner(): lax.ppermute(array, axis, [(i, i ^ 1 << distance) for i in range(lax.axis...  146 us
    ppermute x14, starting transfers between devices, ring_gather(): lax.ppermute(going_down, axis, [(d, (d - 1) % ways) for d in range(ways)])  92.7 us
    reduce_scatter x1, waiting for transfers between devices, forward_update(): lax.psum_scatter(both_sums.astype(jnp.bfloat16), 'front', scatter_dimensi...  80.4 us
    ppermute x23, waiting for transfers between devices, partner(): lax.ppermute(array, axis, [(i, i ^ 1 << distance) for i in range(lax.axis...  75.5 us
    all_gather x3, blocking collectives, backward_front(): lax.all_gather(solved_block, 'front', axis=0, tiled=True)  48.4 us
  transfers between devices with their start and end apart: 58, of which 30 were waited for; matrix products, arithmetic and copies ran while one was open for 0% of the time, Pallas kernels for 0%

profile of v1, /device:TPU:1, one launch (start us, length us, event | category | flops | bytes accessed | tf_op | source)
XLA Modules:
  0.0 1113.0 jit_solution(6875692309507413514)
XLA Ops:
  12.2 39.0 %all_gather.30 = bf16[1024,256]{1,0:T(8,128)(2,1)S(1)} all-gather(bf16[32,256]{1,0:T(8,128)(2,1)S(1)} %fusion.8), channel_id=1, replica_groups=mesh['leaf'=32,'front'=16] {'leaf'}, dimensions={0}, use_global_device_ids=true | all-gather | bytes 540672 | tf_op jit(solution)/shard_map/all_gather | solution.py:42
  52.5 81.3 %reduce-scatter.10.cloned.1.call-done = bf16[32,256]{1,0:T(8,128)(2,1)} async-done(((bf16[512,256]{1,0:T(8,128)(2,1)}), bf16[32,256]{1,0:T(8,128)(2,1)}) %reduce-scatter.10.cloned.1.call-update) | async-done | bytes 16400 | tf_op jit(solution)/shard_map/reduce_scatter | solution.py:68
  134.5 34.5 %all_gather.31 = bf16[1024,256]{1,0:T(8,128)(2,1)S(1)} all-gather(bf16[32,256]{1,0:T(8,128)(2,1)S(1)} %select_convert_fusion.15), channel_id=1, replica_groups=mesh['leaf'=32,'front'=16] {'leaf'}, dimensions={0}, use_global_device_ids=true | all-gather | bytes 540672 | tf_op jit(solution)/shard_map/all_gather | solution.py:42
  174.9 14.5 %collective-permute-done = bf16[256,256]{0,1:T(8,128)(2,1)} collective-permute-done((bf16[256,256]{0,1:T(8,128)(2,1)S(1)}, bf16[256,256]{0,1:T(8,128)(2,1)}, u32[]{:S(2)}, u32[]{:S(2)}) %collective-permute-start) | collective-permute-done | bytes 131104 | tf_op jit(solution)/shard_map/ppermute | solution.py:24
  191.8 80.4 %reduce-scatter.12.cloned.1.call-done = bf16[16,256]{1,0:T(8,128)(2,1)} async-done(((bf16[256,256]{1,0:T(8,128)(2,1)}), bf16[16,256]{1,0:T(8,128)(2,1)}) %reduce-scatter.12.cloned.1.call-update) | async-done | bytes 8208 | tf_op jit(solution)/shard_map/reduce_scatter | solution.py:96
  273.0 34.1 %all_gather.32 = bf16[512,256]{1,0:T(8,128)(2,1)S(1)} all-gather(bf16[16,256]{1,0:T(8,128)(2,1)S(1)} %select_convert_fusion.20), channel_id=1, replica_groups=mesh['leaf'=32,'front'=16] {'leaf'}, dimensions={0}, use_global_device_ids=true | all-gather | bytes 270336 | tf_op jit(solution)/shard_map/all_gather | solution.py:42
  308.2 80.6 %reduce-scatter.14.cloned.1.call-done = bf16[16,256]{1,0:T(8,128)(2,1)} async-done(((bf16[256,256]{1,0:T(8,128)(2,1)}), bf16[16,256]{1,0:T(8,128)(2,1)}) %reduce-scatter.14.cloned.1.call-update) | async-done | bytes 8208 | tf_op jit(solution)/shard_map/reduce_scatter | solution.py:68
  389.6 34.1 %all_gather.33 = bf16[512,256]{1,0:T(8,128)(2,1)S(1)} all-gather(bf16[16,256]{1,0:T(8,128)(2,1)S(1)} %select_convert_fusion.19), channel_id=1, replica_groups=mesh['leaf'=32,'front'=16] {'leaf'}, dimensions={0}, use_global_device_ids=true | all-gather | bytes 270336 | tf_op jit(solution)/shard_map/all_gather | solution.py:42
  424.0 8.9 collective-permute-start.1
  439.5 108.8 %all-reduce.5.cloned.1.call-done = bf16[128,256]{1,0:T(8,128)(2,1)} async-done(((bf16[128,256]{1,0:T(8,128)(2,1)}), bf16[128,256]{1,0:T(8,128)(2,1)}) %all-reduce.5.cloned.1.call-update) | async-done | bytes 65552
  549.1 33.4 %all_gather.34 = bf16[256,256]{1,0:T(8,128)(2,1)S(1)} all-gather(bf16[8,256]{1,0:T(8,128)(2,1)S(1)} %select_convert_fusion.23), channel_id=1, replica_groups=mesh['leaf'=32,'front'=16] {'leaf'}, dimensions={0}, use_global_device_ids=true | all-gather | bytes 135168 | tf_op jit(solution)/shard_map/all_gather | solution.py:42
  584.3 105.7 %all-reduce.7.cloned.1.call-done = bf16[128,256]{1,0:T(8,128)(2,1)} async-done(((bf16[128,256]{1,0:T(8,128)(2,1)}), bf16[128,256]{1,0:T(8,128)(2,1)}) %all-reduce.7.cloned.1.call-update) | async-done | bytes 65552
  690.7 17.5 %all_gather.35 = bf16[128,256]{1,0:T(8,128)(2,1)S(1)} all-gather(bf16[8,256]{1,0:T(8,128)(2,1)S(1)} %select_convert_fusion.22), channel_id=1, replica_groups=mesh['leaf'=32,'front'=16] {'front'}, dimensions={0}, use_global_device_ids=true | all-gather | bytes 69632 | tf_op jit(solution)/shard_map/all_gather | solution.py:112
  709.2 12.5 %collective-permute-start.2 = (bf16[16,8,256]{2,1,0:T(8,128)(2,1)S(1)}, bf16[16,8,256]{2,1,0:T(8,128)(2,1)S(1)}, u32[]{:S(2)}, u32[]{:S(2)}) collective-permute-start(bf16[16,8,256]{2,1,0:T(8,128)(2,1)S(1)} %fusion.26), channel_id=1, source_target_pairs={{0,256},{16,272},{32,288},{48,304},{64,320},{80,336},{96,352},{112... | collective-permute-start | bytes 196616 | tf_op jit(solution)/shard_map/ppermute | solution.py:24
  723.7 7.9 collective-permute-start.3
  745.4 12.3 %collective-permute-start.6 = (bf16[1,8,256]{2,1,0:T(8,128)(2,1)S(1)}, bf16[1,8,256]{2,1,0:T(8,128)(2,1)S(1)}, u32[]{:S(2)}, u32[]{:S(2)}) collective-permute-start(bf16[1,8,256]{2,1,0:T(8,128)(2,1)S(1)} %select_convert_fusion.21), channel_id=1, source_target_pairs={{0,16},{16,0},{32,48},{48,32},{64,80},{80,64},{96,112},{112,96},{1... | collective-permute-start | bytes 12296 | tf_op jit(solution)/shard_map/ppermute | solution.py:24
  758.6 15.9 %all_gather.36 = bf16[128,256]{1,0:T(8,128)(2,1)S(1)} all-gather(bf16[8,256]{1,0:T(8,128)(2,1)S(1)} %fusion.48), channel_id=1, replica_groups=mesh['leaf'=32,'front'=16] {'front'}, dimensions={0}, use_global_device_ids=true | all-gather | bytes 69632 | tf_op jit(solution)/shard_map/all_gather | solution.py:138
  774.5 13.3 %collective-permute-start.7 = (bf16[8,256]{1,0:T(8,128)(2,1)S(1)}, bf16[8,256]{1,0:T(8,128)(2,1)S(1)}, u32[]{:S(2)}, u32[]{:S(2)}) collective-permute-start(bf16[8,256]{1,0:T(8,128)(2,1)S(1)} %fusion.48), channel_id=1, source_target_pairs={{0,256},{16,272},{32,288},{48,304},{64,320},{80,336},{96,352},{112... | collective-permute-start | bytes 12296 | tf_op jit(solution)/shard_map/ppermute | solution.py:24
  799.5 6.7 collective-permute-start.11
  808.1 6.7 collective-permute-start.13
  816.8 6.7 collective-permute-start.15
  825.5 6.7 collective-permute-start.17
  834.2 6.7 collective-permute-start.19
  842.8 6.7 collective-permute-start.21
  878.3 16.8 %collective-permute-start.26 = (bf16[1,16,256]{2,1,0:T(8,128)(2,1)S(1)}, bf16[1,16,256]{2,1,0:T(8,128)(2,1)S(1)}, u32[]{:S(2)}, u32[]{:S(2)}) collective-permute-start(bf16[1,16,256]{2,1,0:T(8,128)(2,1)S(1)} %select_convert_fusion.17), channel_id=1, source_target_pairs={{0,16},{16,0},{32,48},{48,32},{64,80},{80,64},{96,112},{112,96},{1... | collective-permute-start | bytes 24584 | tf_op jit(solution)/shard_map/ppermute | solution.py:24
  896.1 15.4 %all_gather.37 = bf16[256,256]{1,0:T(8,128)(2,1)S(1)} all-gather(bf16[16,256]{1,0:T(8,128)(2,1)S(1)} %fusion.39), channel_id=1, replica_groups=mesh['leaf'=32,'front'=16] {'front'}, dimensions={0}, use_global_device_ids=true | all-gather | bytes 139264 | tf_op jit(solution)/shard_map/all_gather | solution.py:112
  932.8 10.0 collective-permute-start.30
  943.7 18.3 %all_gather.38 = bf16[256,256]{1,0:T(8,128)(2,1)S(1)} all-gather(bf16[16,256]{1,0:T(8,128)(2,1)S(1)} %fusion.37), channel_id=1, replica_groups=mesh['leaf'=32,'front'=16] {'front'}, dimensions={0}, use_global_device_ids=true | all-gather | bytes 139264 | tf_op jit(solution)/shard_map/all_gather | solution.py:138
  998.2 6.7 collective-permute-start.39
  1050.3 16.0 %collective-permute-start.49 = (bf16[1,32,256]{2,1,0:T(8,128)(2,1)S(1)}, bf16[1,32,256]{2,1,0:T(8,128)(2,1)S(1)}, u32[]{:S(2)}, u32[]{:S(2)}) collective-permute-start(bf16[1,32,256]{2,1,0:T(8,128)(2,1)S(1)} %select_convert_fusion.11), channel_id=1, source_target_pairs={{0,16},{16,0},{32,48},{48,32},{64,80},{80,64},{96,112},{112,96},{1... | collective-permute-start | bytes 49160 | tf_op jit(solution)/shard_map/ppermute | solution.py:24
  1067.1 15.5 %all_gather.39 = bf16[512,256]{1,0:T(8,128)(2,1)S(1)} all-gather(bf16[32,256]{1,0:T(8,128)(2,1)S(1)} %fusion.36), channel_id=1, replica_groups=mesh['leaf'=32,'front'=16] {'front'}, dimensions={0}, use_global_device_ids=true | all-gather | bytes 278528 | tf_op jit(solution)/shard_map/all_gather | solution.py:112
  1093.7 9.7 collective-permute-start.52
  (253 shorter events, 213.1 us)
Async XLA Ops:
  7.2 126.5 %reduce-scatter.10.cloned.1.call-start = ((), (), s32[]{:S(2)}) async-start(), calls=%async_computation.3 | async-start | bytes 278528 | tf_op jit(solution)/shard_map/reduce_scatter | solution.py:68
  52.3 219.9 %reduce-scatter.12.cloned.1.call-start = ((), (), s32[]{:S(2)}) async-start(), calls=%async_computation.4 | async-start | bytes 139264 | tf_op jit(solution)/shard_map/reduce_scatter | solution.py:96
  170.0 19.4 %collective-permute-start = (bf16[256,256]{0,1:T(8,128)(2,1)S(1)}, bf16[256,256]{0,1:T(8,128)(2,1)}, u32[]{:S(2)}, u32[]{:S(2)}) collective-permute-start(bf16[256,256]{0,1:T(8,128)(2,1)S(1)} %bitcast.156), channel_id=1, source_target_pairs={{0,128},{16,144},{32,160},{48,176},{64,192},{80,208},{96,224},{112... | collective-permute-start | bytes 393224 | tf_op jit(solution)/shard_map/ppermute | solution.py:24
  191.1 197.7 %reduce-scatter.14.cloned.1.call-start = ((), (), s32[]{:S(2)}) async-start(), calls=%async_computation.5 | async-start | bytes 139264 | tf_op jit(solution)/shard_map/reduce_scatter | solution.py:68
  308.1 240.2 %all-reduce.5.cloned.1.call-start = ((), (), s32[]{:S(2)}) async-start(), calls=%async_computation.6 | async-start | bytes 131072
  424.0 14.2 %collective-permute-start.1 = (bf16[128,256]{1,0:T(8,128)(2,1)S(1)}, bf16[128,256]{1,0:T(8,128)(2,1)S(1)}, u32[]{:S(2)}, u32[]{:S(2)}) collective-permute-start(bf16[128,256]{1,0:T(8,128)(2,1)S(1)} %fusion.25), channel_id=1, source_target_pairs={{0,256},{16,272},{32,288},{48,304},{64,320},{80,336},{96,352},{112... | collective-permute-start | bytes 196616 | tf_op jit(solution)/shard_map/ppermute | solution.py:24
  438.8 251.2 %all-reduce.7.cloned.1.call-start = ((), (), s32[]{:S(2)}) async-start(), calls=%async_computation.7 | async-start | bytes 131072
  709.2 14.5 %collective-permute-start.2 = (bf16[16,8,256]{2,1,0:T(8,128)(2,1)S(1)}, bf16[16,8,256]{2,1,0:T(8,128)(2,1)S(1)}, u32[]{:S(2)}, u32[]{:S(2)}) collective-permute-start(bf16[16,8,256]{2,1,0:T(8,128)(2,1)S(1)} %fusion.26), channel_id=1, source_target_pairs={{0,256},{16,272},{32,288},{48,304},{64,320},{80,336},{96,352},{112... | collective-permute-start | bytes 196616 | tf_op jit(solution)/shard_map/ppermute | solution.py:24
  723.7 11.9 %collective-permute-start.3 = (bf16[8,8,256]{2,1,0:T(8,128)(2,1)S(1)}, bf16[8,8,256]{2,1,0:T(8,128)(2,1)S(1)}, u32[]{:S(2)}, u32[]{:S(2)}) collective-permute-start(bf16[8,8,256]{2,1,0:T(8,128)(2,1)S(1)} %select_convert_fusion.9), channel_id=1, source_target_pairs={{0,128},{16,144},{32,160},{48,176},{64,192},{80,208},{96,224},{112... | collective-permute-start | bytes 98312 | tf_op jit(solution)/shard_map/ppermute | solution.py:24
  745.4 13.1 %collective-permute-start.6 = (bf16[1,8,256]{2,1,0:T(8,128)(2,1)S(1)}, bf16[1,8,256]{2,1,0:T(8,128)(2,1)S(1)}, u32[]{:S(2)}, u32[]{:S(2)}) collective-permute-start(bf16[1,8,256]{2,1,0:T(8,128)(2,1)S(1)} %select_convert_fusion.21), channel_id=1, source_target_pairs={{0,16},{16,0},{32,48},{48,32},{64,80},{80,64},{96,112},{112,96},{1... | collective-permute-start | bytes 12296 | tf_op jit(solution)/shard_map/ppermute | solution.py:24
  774.5 14.3 %collective-permute-start.7 = (bf16[8,256]{1,0:T(8,128)(2,1)S(1)}, bf16[8,256]{1,0:T(8,128)(2,1)S(1)}, u32[]{:S(2)}, u32[]{:S(2)}) collective-permute-start(bf16[8,256]{1,0:T(8,128)(2,1)S(1)} %fusion.48), channel_id=1, source_target_pairs={{0,256},{16,272},{32,288},{48,304},{64,320},{80,336},{96,352},{112... | collective-permute-start | bytes 12296 | tf_op jit(solution)/shard_map/ppermute | solution.py:24
  797.5 8.7 collective-permute-start.10
  799.5 8.7 collective-permute-start.11
  806.2 8.7 collective-permute-start.12
  808.1 8.7 collective-permute-start.13
  814.9 8.7 collective-permute-start.14
  816.8 8.7 collective-permute-start.15
  834.2 8.7 collective-permute-start.19
  840.9 8.7 collective-permute-start.20
  842.8 8.7 collective-permute-start.21
  857.4 10.5 collective-permute-start.23
  878.3 17.6 %collective-permute-start.26 = (bf16[1,16,256]{2,1,0:T(8,128)(2,1)S(1)}, bf16[1,16,256]{2,1,0:T(8,128)(2,1)S(1)}, u32[]{:S(2)}, u32[]{:S(2)}) collective-permute-start(bf16[1,16,256]{2,1,0:T(8,128)(2,1)S(1)} %select_convert_fusion.17), channel_id=1, source_target_pairs={{0,16},{16,0},{32,48},{48,32},{64,80},{80,64},{96,112},{112,96},{1... | collective-permute-start | bytes 24584 | tf_op jit(solution)/shard_map/ppermute | solution.py:24
  911.7 10.1 collective-permute-start.27
  932.8 10.8 collective-permute-start.30
  972.2 8.7 collective-permute-start.33
  989.6 8.7 collective-permute-start.37
  996.3 8.7 collective-permute-start.38
  998.2 8.7 collective-permute-start.39
  1005.0 8.7 collective-permute-start.40
  1024.3 8.7 collective-permute-start.45
  1050.3 16.8 %collective-permute-start.49 = (bf16[1,32,256]{2,1,0:T(8,128)(2,1)S(1)}, bf16[1,32,256]{2,1,0:T(8,128)(2,1)S(1)}, u32[]{:S(2)}, u32[]{:S(2)}) collective-permute-start(bf16[1,32,256]{2,1,0:T(8,128)(2,1)S(1)} %select_convert_fusion.11), channel_id=1, source_target_pairs={{0,16},{16,0},{32,48},{48,32},{64,80},{80,64},{96,112},{112,96},{1... | collective-permute-start | bytes 49160 | tf_op jit(solution)/shard_map/ppermute | solution.py:24
  1093.7 10.5 collective-permute-start.52
  (45 other events, 1995.9 us)
Sparse Core Ops, SparseCore 0:
  52.5 81.2 reduce-scatter.9
  191.2 80.9 reduce-scatter.11
  308.2 80.5 reduce-scatter.13
  438.9 109.3 all-reduce.4
  584.4 105.5 all-reduce.6
